TPU v7x, 32 devices: a whole 2x2x4 slice. The times are simulated.
32 devices in a mesh: sector: 8 (over y, x, core), term: 4 (over z).
Axes of the slice: x: 2, y: 2, z: 4, core: 2. Of those that a mesh axis runs over, the one named last changes fastest.
Arguments:
- wave: float32 [8, 512, 512], P('sector', 'term'), may hold values from -12 to 12
- left_ops: bfloat16 [16, 8, 512, 512], P('term', 'sector'), may hold values from -4 to 4
- right_ops: bfloat16 [16, 8, 512, 512], P('term', 'sector'), may hold values from -4 to 4
- charges: int32 [16], replicated, may hold values from -1 to 1, as said below
- diag: float32 [8, 512, 512], P('sector', 'term'), may hold values from 0.5 to 8
Outputs:
- psi_out: float32 [8, 512, 512], P('sector', 'term')
Inputs may be any that keep to these rules, and one draw needn't show every extreme that they name: `charges`: exactly (17) // 2 terms have charge 0; at least one term has charge 1 and at least one has charge -1.
All inputs are finite; a program needn't handle non-finite values.
Results may differ from a plain program's by a relative error of at most 0.0085.
Values may be sent and summed in bfloat16 or wider, within the bound.
No kernel may reach another device: no remote copies, remote signals or barrier semaphores. Data moves between devices by JAX's collectives and lax.ppermute only.
A program may use at most 64 MiB of HBM per device.

v0:
```python
import jax
import jax.numpy as jnp
from jax import lax
from jax.sharding import PartitionSpec as P

STEPS = 3


def from_behind(value, axis, steps):
    count = lax.axis_size(axis)
    leading, last = (max(0, -steps), min(count, count - steps))
    return lax.ppermute(value, axis, [(source, source + steps) for source in range(leading, last)])


def apply_terms(left_ops, right_ops, my_charges, own, lower, upper):
    stacked = jnp.stack([upper, own, lower])
    picked = stacked[my_charges + 1]
    inner = jnp.einsum(
        "tij,tjk->tik", left_ops[:, 0], picked, preferred_element_type=jnp.float32
    ).astype(jnp.bfloat16)
    image = jnp.einsum("tij,tkj->tik", inner, right_ops[:, 0], preferred_element_type=jnp.float32)
    return jnp.sum(image, axis=0)


def per_device(wave, left_ops, right_ops, charges, diag):
    per_dev = left_ops.shape[0]
    my_charges = lax.dynamic_slice_in_dim(charges, lax.axis_index("term") * per_dev, per_dev)
    psi, full_diag = (
        lax.all_gather(wave[0], "term", axis=0, tiled=True),
        lax.all_gather(diag[0], "term", axis=0, tiled=True),
    )
    for step in range(STEPS):
        wb = psi.astype(jnp.bfloat16)
        lower = from_behind(wb, "sector", 1)
        upper = from_behind(wb, "sector", -1)
        partial_image = apply_terms(left_ops, right_ops, my_charges, wb, lower, upper)
        hpsi = lax.psum(partial_image, "term")
        cross, square = lax.psum((jnp.sum(psi * hpsi), jnp.sum(psi * psi)), "sector")
        theta = cross / square
        fresh = psi - (hpsi - theta * psi) / jnp.maximum(jnp.abs(full_diag - theta), 1.0)
        total = lax.psum(jnp.sum(fresh * fresh), "sector")
        psi = fresh / jnp.sqrt(total / (lax.axis_size("sector") * fresh.size) + 1e-06)
    rows_dev = wave.shape[1]
    result = lax.dynamic_slice_in_dim(psi, lax.axis_index("term") * rows_dev, rows_dev, 0)
    return result[None]


def solution(mesh):
    in_specs = (
        P("sector", "term", None),
        P("term", "sector", None, None),
        P("term", "sector", None, None),
        P(),
        P("sector", "term", None),
    )
    out_specs = P("sector", "term", None)
    return jax.shard_map(
        per_device, mesh=mesh, in_specs=in_specs, out_specs=out_specs, check_vma=False
    )
```

profile of v0, /device:TPU:0, one launch (start us, length us, event | category | flops | bytes accessed | tf_op | source)
XLA Modules:
  0.0 397.1 jit_solution(17423861717904664301)
XLA Ops:
  7.3 32.3 %all-gather.5.cloned.1.call-done = f32[1,512,512]{2,1,0:T(8,128)} async-done(((f32[1,128,512]{2,1,0:T(8,128)}), f32[1,512,512]{2,1,0:T(8,128)}) %all-gather.5.cloned.1.call-update) | async-done | bytes 1048592 | tf_op jit(solution)/shard_map/all_gather | solution.py:29
  39.6 2.2 bitcast_convert_fusion
  41.8 2.1 collective-permute-start.1
  46.0 2.9 collective-permute-done
  49.0 2.5 pad_maximum_fusion
  51.5 3.4 gather_fusion
  54.9 5.5 %fusion.30 = f32[512,512]{1,0:T(8,128)} fusion(bf16[4,1,512,512]{3,2,1,0:T(8,128)(2,1)S(1)} %copy-done, bf16[4,512,512]{2,1,0:T(8,128)(2,1)} %gather_fusion, bf16[4,1,512,512]{3,2,1,0:T(8,128)(2,1)} %param.6), kind=kOutput, calls=%fused_computation.24 | convolution fusion | flops 2148532224 | bytes 7340032 | tf_op jit(solution)/shard_map/tij,tkj->tik/dot_general | solution.py:21
  61.3 59.4 %all-reduce.7.cloned.1.call-done = f32[512,512]{1,0:T(8,128)} async-done(((f32[512,512]{1,0:T(8,128)}), f32[512,512]{1,0:T(8,128)}) %all-reduce.7.cloned.1.call-update) | async-done | bytes 1048592 | tf_op jit(solution)/shard_map/psum | solution.py:37
  120.6 2.2 fusion.55
  122.8 14.7 %all-reduce.2 = (f32[]{:T(128)}, f32[]{:T(128)}) all-reduce(f32[]{:T(128)} %get-tuple-element.10, f32[]{:T(128)} %get-tuple-element.9), channel_id=1, replica_groups=mesh['sector'=8,'term'=4] {'sector'}, use_global_device_ids=true, to_apply=%region_2.0 | all-reduce | flops 2 | bytes 16 | tf_op jit(solution)/shard_map/psum | solution.py:38
  138.8 10.7 %all-gather.7.cloned.1.call-done = f32[1,512,512]{2,1,0:T(8,128)} async-done(((f32[1,128,512]{2,1,0:T(8,128)}), f32[1,512,512]{2,1,0:T(8,128)}) %all-gather.7.cloned.1.call-update) | async-done | bytes 1048592 | tf_op jit(solution)/shard_map/all_gather | solution.py:30
  149.5 2.8 multiply_reduce_fusion.6
  152.4 13.7 %psum.87 = f32[]{:T(128)} all-reduce(f32[]{:T(128)} %get-tuple-element.21), channel_id=1, replica_groups=mesh['sector'=8,'term'=4] {'sector'}, use_global_device_ids=true, to_apply=%region_6.0 | all-reduce | flops 1 | bytes 8 | tf_op jit(solution)/shard_map/psum | solution.py:41
  169.7 2.3 collective-permute-done.2
  173.4 3.4 gather_fusion.1
  176.8 5.5 %fusion.37 = f32[512,512]{1,0:T(8,128)} fusion(bf16[4,1,512,512]{3,2,1,0:T(8,128)(2,1)S(1)} %copy-done, bf16[4,512,512]{2,1,0:T(8,128)(2,1)} %gather_fusion.1, bf16[4,1,512,512]{3,2,1,0:T(8,128)(2,1)} %param.6), kind=kOutput, calls=%fused_computation.25 | convolution fusion | flops 2148532224 | bytes 7340032 | tf_op jit(solution)/shard_map/tij,tkj->tik/dot_general | solution.py:21
  182.4 60.9 %all-reduce.9.cloned.1.call-done = f32[512,512]{1,0:T(8,128)} async-done(((f32[512,512]{1,0:T(8,128)}), f32[512,512]{1,0:T(8,128)}) %all-reduce.9.cloned.1.call-update) | async-done | bytes 1048592 | tf_op jit(solution)/shard_map/psum | solution.py:37
  243.3 2.2 multiply_reduce_fusion.4
  245.5 14.3 %all-reduce.1 = (f32[]{:T(128)}, f32[]{:T(128)}) all-reduce(f32[]{:T(128)} %get-tuple-element.8, f32[]{:T(128)} %get-tuple-element.7), channel_id=1, replica_groups=mesh['sector'=8,'term'=4] {'sector'}, use_global_device_ids=true, to_apply=%region_9.0 | all-reduce | flops 2 | bytes 16 | tf_op jit(solution)/shard_map/psum | solution.py:38
  261.1 3.6 multiply_reduce_fusion.3
  264.6 12.4 %psum.91 = f32[]{:T(128)} all-reduce(f32[]{:T(128)} %get-tuple-element.19), channel_id=1, replica_groups=mesh['sector'=8,'term'=4] {'sector'}, use_global_device_ids=true, to_apply=%region_13.0 | all-reduce | flops 1 | bytes 8 | tf_op jit(solution)/shard_map/psum | solution.py:41
  277.8 1.3 fusion.59
  279.1 1.8 collective-permute-start.5
  282.4 2.3 collective-permute-done.4
  286.0 3.4 gather_fusion.2
  289.5 5.5 %fusion.44 = f32[512,512]{1,0:T(8,128)} fusion(bf16[4,1,512,512]{3,2,1,0:T(8,128)(2,1)S(1)} %copy-done, bf16[4,512,512]{2,1,0:T(8,128)(2,1)} %gather_fusion.2, bf16[4,1,512,512]{3,2,1,0:T(8,128)(2,1)} %param.6), kind=kOutput, calls=%fused_computation.26 | convolution fusion | flops 2148532224 | bytes 7340032 | tf_op jit(solution)/shard_map/tij,tkj->tik/dot_general | solution.py:21
  295.0 59.5 %all-reduce.11.cloned.1.call-done = f32[512,512]{1,0:T(8,128)} async-done(((f32[512,512]{1,0:T(8,128)}), f32[512,512]{1,0:T(8,128)}) %all-reduce.11.cloned.1.call-update) | async-done | bytes 1048592 | tf_op jit(solution)/shard_map/psum | solution.py:37
  354.5 2.2 multiply_reduce_fusion.1
  356.7 14.3 %all-reduce = (f32[]{:T(128)}, f32[]{:T(128)}) all-reduce(f32[]{:T(128)} %get-tuple-element.6, f32[]{:T(128)} %get-tuple-element.5), channel_id=1, replica_groups=mesh['sector'=8,'term'=4] {'sector'}, use_global_device_ids=true, to_apply=%region_16.0 | all-reduce | flops 2 | bytes 16 | tf_op jit(solution)/shard_map/psum | solution.py:38
  372.3 3.6 multiply_reduce_fusion
  375.8 12.4 %psum.95 = f32[]{:T(128)} all-reduce(f32[]{:T(128)} %get-tuple-element.17), channel_id=1, replica_groups=mesh['sector'=8,'term'=4] {'sector'}, use_global_device_ids=true, to_apply=%region_20.0 | all-reduce | flops 1 | bytes 8 | tf_op jit(solution)/shard_map/psum | solution.py:41
  388.9 1.7 fusion.57
  (31 shorter events, 10.7 us)
Async XLA Ops:
  6.5 48.4 %copy-start = (bf16[4,1,512,512]{3,2,1,0:T(8,128)(2,1)S(1)}, bf16[4,1,512,512]{3,2,1,0:T(8,128)(2,1)}, u32[]{:S(2)}) copy-start(bf16[4,1,512,512]{3,2,1,0:T(8,128)(2,1)} %param.7) | copy-start | bytes 6291460
  6.5 33.1 %all-gather.5.cloned.1.call-start = ((), (), s32[]{:S(2)}) async-start(), calls=%async_computation.3 | async-start | bytes 1310720 | tf_op jit(solution)/shard_map/all_gather | solution.py:29
  7.3 113.4 %all-reduce.7.cloned.1.call-start = ((), (), s32[]{:S(2)}) async-start(), calls=%async_computation | async-start | bytes 2097152 | tf_op jit(solution)/shard_map/psum | solution.py:37
  39.6 6.3 %copy-start.2 = (f32[1,512,512]{2,1,0:T(8,128)S(1)}, f32[1,512,512]{2,1,0:T(8,128)}, u32[]{:S(2)}) copy-start(f32[1,512,512]{2,1,0:T(8,128)} %all-gather.5.cloned.1.call-done) | copy-start | bytes 3145732
  41.8 4.2 %collective-permute-start.1 = (bf16[512,512]{1,0:T(8,128)(2,1)}, bf16[512,512]{1,0:T(8,128)(2,1)}, u32[]{:S(2)}, u32[]{:S(2)}) collective-permute-start(bf16[512,512]{1,0:T(8,128)(2,1)} %bitcast_convert_fusion), channel_id=1, source_target_pairs={{0,4},{4,8},{8,12},{12,16},{16,20},{20,24},{24,28},{1,5},{5,9},{9,... | collective-permute-start | bytes 1572872 | tf_op jit(solution)/shard_map/ppermute | solution.py:12
  43.9 5.0 %collective-permute-start = (bf16[512,512]{1,0:T(8,128)(2,1)}, bf16[512,512]{1,0:T(8,128)(2,1)}, u32[]{:S(2)}, u32[]{:S(2)}) collective-permute-start(bf16[512,512]{1,0:T(8,128)(2,1)} %bitcast_convert_fusion), channel_id=1, source_target_pairs={{4,0},{8,4},{12,8},{16,12},{20,16},{24,20},{28,24},{5,1},{9,5},{13... | collective-permute-start | bytes 1572872 | tf_op jit(solution)/shard_map/ppermute | solution.py:12
  60.5 89.0 %all-gather.7.cloned.1.call-start = ((), (), s32[]{:S(2)}) async-start(), calls=%async_computation.4 | async-start | bytes 1310720 | tf_op jit(solution)/shard_map/all_gather | solution.py:30
  61.2 182.1 %all-reduce.9.cloned.1.call-start = ((), (), s32[]{:S(2)}) async-start(), calls=%async_computation.1 | async-start | bytes 2097152 | tf_op jit(solution)/shard_map/psum | solution.py:37
  166.9 2.8 collective-permute-start.3
  168.2 3.8 collective-permute-start.2
  182.4 172.1 %all-reduce.11.cloned.1.call-start = ((), (), s32[]{:S(2)}) async-start(), calls=%async_computation.2 | async-start | bytes 2097152 | tf_op jit(solution)/shard_map/psum | solution.py:37
  264.6 17.6 %copy-start.1 = (f32[512,512]{1,0:T(8,128)S(1)}, f32[512,512]{1,0:T(8,128)}, u32[]{:S(2)}) copy-start(f32[512,512]{1,0:T(8,128)} %get-tuple-element.20) | copy-start | bytes 3145732
  279.1 3.3 collective-permute-start.5
  280.9 3.8 collective-permute-start.4
Sparse Core Ops, SparseCore 0:
  8.9 30.6 all-gather.4
  60.6 59.9 all-reduce.6
  122.2 27.2 all-gather.6
  182.5 60.7 all-reduce.8
  295.2 59.3 all-reduce.10
where the time goes:
time: 398 us; the launch traced here: 397 us
  waiting for transfers between devices  232 us (58%)
  blocking collectives  81.9 us (21%)
  other arithmetic  28 us (7%)
  between operations  19.1 us (5%)
  matrix products  16.6 us (4%)
  local copies, waits for them, and re-layouts  10.3 us (3%)
  starting transfers between devices  9.25 us (2%)
    psum x3, waiting for transfers between devices, per_device(): hpsi = lax.psum(partial_image, 'term')  180 us
    psum x3, blocking collectives, per_device(): lax.psum((jnp.sum(psi * hpsi), jnp.sum(psi * psi)), 'sector')  43.4 us
    psum x3, blocking collectives, per_device(): total = lax.psum(jnp.sum(fresh * fresh), 'sector')  38.6 us
    all_gather x1, waiting for transfers between devices, per_device(): lax.all_gather(wave[0], 'term', axis=0, tiled=True)  32.3 us
    dot_general x3, matrix products, apply_terms(): jnp.einsum('tij,tkj->tik', inner, right_ops[:, 0], preferred_element_type...  16.6 us
    all_gather x1, waiting for transfers between devices, per_device(): lax.all_gather(diag[0], 'term', axis=0, tiled=True)  10.7 us
    gather x3, local copies, waits for them, and re-layouts, apply_terms(): picked = stacked[my_charges + 1]  10.3 us
    reduce_sum x3, other arithmetic, per_device(): total = lax.psum(jnp.sum(fresh * fresh), 'sector')  9.95 us
  transfers between devices with their start and end apart: 11, of which 10 were waited for; matrix products, arithmetic and copies ran while one was open for 1% of the time, Pallas kernels for 0%

commit v1 on v0

--- a/solution.py
+++ b/solution.py
@@ -34,7 +34,8 @@
         lower = from_behind(wb, "sector", 1)
         upper = from_behind(wb, "sector", -1)
         partial_image = apply_terms(left_ops, right_ops, my_charges, wb, lower, upper)
-        hpsi = lax.psum(partial_image, "term")
+        halves_produce = lambda frame: jnp.sum(lax.all_gather(frame, "term"), axis=0)
+        hpsi = halves_produce(partial_image)
         cross, square = lax.psum((jnp.sum(psi * hpsi), jnp.sum(psi * psi)), "sector")
         theta = cross / square
         fresh = psi - (hpsi - theta * psi) / jnp.maximum(jnp.abs(full_diag - theta), 1.0)

time: 398 us -> 490 us (1.23)
  waiting for transfers between devices: 232 us -> 313 us
  other arithmetic: 28 us -> 39.4 us
    all_gather x0 -> x3, waiting for transfers between devices: none -> 266 us  [per_device(): lax.all_gather(frame, 'term')]
    psum x3 -> x0, waiting for transfers between devices: 180 us -> none  [per_device(): hpsi = lax.psum(partial_image, 'term')]
    reduce_sum x0 -> x3, other arithmetic: none -> 11.4 us  [per_device(): jnp.sum(lax.all_gather(frame, 'term'), axis=0)]
where the time goes in v1:
time: 490 us
  waiting for transfers between devices  313 us (64%)
  blocking collectives  81.3 us (17%)
  other arithmetic  39.4 us (8%)
  between operations  19.1 us (4%)
  matrix products  16.7 us (3%)
  local copies, waits for them, and re-layouts  10.3 us (2%)
  starting transfers between devices  9.25 us (2%)
    all_gather x3, waiting for transfers between devices, per_device(): lax.all_gather(frame, 'term')  266 us
    psum x3, blocking collectives, per_device(): lax.psum((jnp.sum(psi * hpsi), jnp.sum(psi * psi)), 'sector')  42.7 us
    psum x3, blocking collectives, per_device(): total = lax.psum(jnp.sum(fresh * fresh), 'sector')  38.6 us
    all_gather x1, waiting for transfers between devices, per_device(): lax.all_gather(wave[0], 'term', axis=0, tiled=True)  32.3 us
    dot_general x3, matrix products, apply_terms(): jnp.einsum('tij,tkj->tik', inner, right_ops[:, 0], preferred_element_type...  16.7 us
    reduce_sum x3, other arithmetic, per_device(): jnp.sum(lax.all_gather(frame, 'term'), axis=0)  11.4 us
    gather x3, local copies, waits for them, and re-layouts, apply_terms(): picked = stacked[my_charges + 1]  10.3 us
    reduce_sum x3, other arithmetic, per_device(): total = lax.psum(jnp.sum(fresh * fresh), 'sector')  9.92 us
  transfers between devices with their start and end apart: 11, of which 10 were waited for; matrix products, arithmetic and copies ran while one was open for 1% of the time, Pallas kernels for 0%

profile of v1, /device:TPU:0, one launch (start us, length us, event | category | flops | bytes accessed | tf_op | source)
XLA Modules:
  0.0 489.5 jit_solution(11015255673384898556)
XLA Ops:
  7.3 32.3 %all-gather.11.cloned.1.call-done = f32[1,512,512]{2,1,0:T(8,128)} async-done(((f32[1,128,512]{2,1,0:T(8,128)}), f32[1,512,512]{2,1,0:T(8,128)}) %all-gather.11.cloned.1.call-update) | async-done | bytes 1048592 | tf_op jit(solution)/shard_map/all_gather | solution.py:29
  39.6 2.2 bitcast_convert_fusion
  41.8 2.1 collective-permute-start.1
  46.1 2.9 collective-permute-done
  49.0 2.5 pad_maximum_fusion
  51.5 3.4 gather_fusion
  54.9 5.6 %fusion.30 = f32[512,512]{1,0:T(8,128)} fusion(bf16[4,1,512,512]{3,2,1,0:T(8,128)(2,1)S(1)} %copy-done, bf16[4,512,512]{2,1,0:T(8,128)(2,1)} %gather_fusion, bf16[4,1,512,512]{3,2,1,0:T(8,128)(2,1)} %param.6), kind=kOutput, calls=%fused_computation.24 | convolution fusion | flops 2148532224 | bytes 7340032 | tf_op jit(solution)/shard_map/tij,tkj->tik/dot_general | solution.py:21
  61.3 88.2 %all-gather.13.cloned.1.call-done = f32[2048,512]{1,0:T(8,128)} async-done(((f32[512,512]{1,0:T(8,128)}), f32[2048,512]{1,0:T(8,128)}) %all-gather.13.cloned.1.call-update) | async-done | bytes 4194320 | tf_op jit(solution)/shard_map/all_gather | solution.py:37
  149.5 3.8 reduce_sum.120
  153.3 2.2 fusion.55
  155.5 14.5 %all-reduce.2 = (f32[]{:T(128)}, f32[]{:T(128)}) all-reduce(f32[]{:T(128)} %get-tuple-element.10, f32[]{:T(128)} %get-tuple-element.9), channel_id=1, replica_groups=mesh['sector'=8,'term'=4] {'sector'}, use_global_device_ids=true, to_apply=%region_2.0 | all-reduce | flops 2 | bytes 16 | tf_op jit(solution)/shard_map/psum | solution.py:39
  171.3 6.3 %all-gather.15.cloned.1.call-done = f32[1,512,512]{2,1,0:T(8,128)} async-done(((f32[1,128,512]{2,1,0:T(8,128)}), f32[1,512,512]{2,1,0:T(8,128)}) %all-gather.15.cloned.1.call-update) | async-done | bytes 1048592 | tf_op jit(solution)/shard_map/all_gather | solution.py:30
  177.6 2.8 multiply_reduce_fusion.6
  180.5 13.7 %psum.65 = f32[]{:T(128)} all-reduce(f32[]{:T(128)} %get-tuple-element.21), channel_id=1, replica_groups=mesh['sector'=8,'term'=4] {'sector'}, use_global_device_ids=true, to_apply=%region_6.0 | all-reduce | flops 1 | bytes 8 | tf_op jit(solution)/shard_map/psum | solution.py:42
  197.9 2.3 collective-permute-done.2
  201.5 3.4 gather_fusion.1
  204.9 5.6 %fusion.37 = f32[512,512]{1,0:T(8,128)} fusion(bf16[4,1,512,512]{3,2,1,0:T(8,128)(2,1)S(1)} %copy-done, bf16[4,512,512]{2,1,0:T(8,128)(2,1)} %gather_fusion.1, bf16[4,1,512,512]{3,2,1,0:T(8,128)(2,1)} %param.6), kind=kOutput, calls=%fused_computation.25 | convolution fusion | flops 2148532224 | bytes 7340032 | tf_op jit(solution)/shard_map/tij,tkj->tik/dot_general | solution.py:21
  210.6 89.8 %all-gather.17.cloned.1.call-done = f32[2048,512]{1,0:T(8,128)} async-done(((f32[512,512]{1,0:T(8,128)}), f32[2048,512]{1,0:T(8,128)}) %all-gather.17.cloned.1.call-update) | async-done | bytes 4194320 | tf_op jit(solution)/shard_map/all_gather | solution.py:37
  300.3 3.8 reduce_sum.124
  304.1 2.2 multiply_reduce_fusion.4
  306.3 14.1 %all-reduce.1 = (f32[]{:T(128)}, f32[]{:T(128)}) all-reduce(f32[]{:T(128)} %get-tuple-element.8, f32[]{:T(128)} %get-tuple-element.7), channel_id=1, replica_groups=mesh['sector'=8,'term'=4] {'sector'}, use_global_device_ids=true, to_apply=%region_9.0 | all-reduce | flops 2 | bytes 16 | tf_op jit(solution)/shard_map/psum | solution.py:39
  321.7 3.5 multiply_reduce_fusion.3
  325.2 12.4 %psum.68 = f32[]{:T(128)} all-reduce(f32[]{:T(128)} %get-tuple-element.19), channel_id=1, replica_groups=mesh['sector'=8,'term'=4] {'sector'}, use_global_device_ids=true, to_apply=%region_13.0 | all-reduce | flops 1 | bytes 8 | tf_op jit(solution)/shard_map/psum | solution.py:42
  342.9 2.3 collective-permute-done.4
  346.6 3.4 gather_fusion.2
  350.0 5.6 %fusion.44 = f32[512,512]{1,0:T(8,128)} fusion(bf16[4,1,512,512]{3,2,1,0:T(8,128)(2,1)S(1)} %copy-done, bf16[4,512,512]{2,1,0:T(8,128)(2,1)} %gather_fusion.2, bf16[4,1,512,512]{3,2,1,0:T(8,128)(2,1)} %param.6), kind=kOutput, calls=%fused_computation.26 | convolution fusion | flops 2148532224 | bytes 7340032 | tf_op jit(solution)/shard_map/tij,tkj->tik/dot_general | solution.py:21
  355.6 87.7 %all-gather.19.cloned.1.call-done = f32[2048,512]{1,0:T(8,128)} async-done(((f32[512,512]{1,0:T(8,128)}), f32[2048,512]{1,0:T(8,128)}) %all-gather.19.cloned.1.call-update) | async-done | bytes 4194320 | tf_op jit(solution)/shard_map/all_gather | solution.py:37
  443.3 3.8 reduce_sum.128
  447.1 2.2 multiply_reduce_fusion.1
  449.3 14.1 %all-reduce = (f32[]{:T(128)}, f32[]{:T(128)}) all-reduce(f32[]{:T(128)} %get-tuple-element.6, f32[]{:T(128)} %get-tuple-element.5), channel_id=1, replica_groups=mesh['sector'=8,'term'=4] {'sector'}, use_global_device_ids=true, to_apply=%region_16.0 | all-reduce | flops 2 | bytes 16 | tf_op jit(solution)/shard_map/psum | solution.py:39
  464.7 3.5 multiply_reduce_fusion
  468.2 12.4 %psum.71 = f32[]{:T(128)} all-reduce(f32[]{:T(128)} %get-tuple-element.17), channel_id=1, replica_groups=mesh['sector'=8,'term'=4] {'sector'}, use_global_device_ids=true, to_apply=%region_20.0 | all-reduce | flops 1 | bytes 8 | tf_op jit(solution)/shard_map/psum | solution.py:42
  (34 shorter events, 15.6 us)
Async XLA Ops:
  6.5 48.4 %copy-start = (bf16[4,1,512,512]{3,2,1,0:T(8,128)(2,1)S(1)}, bf16[4,1,512,512]{3,2,1,0:T(8,128)(2,1)}, u32[]{:S(2)}) copy-start(bf16[4,1,512,512]{3,2,1,0:T(8,128)(2,1)} %param.7) | copy-start | bytes 6291460
  6.5 33.1 %all-gather.11.cloned.1.call-start = ((), (), s32[]{:S(2)}) async-start(), calls=%async_computation | async-start | bytes 1310720 | tf_op jit(solution)/shard_map/all_gather | solution.py:29
  7.3 142.3 %all-gather.13.cloned.1.call-start = ((), (), s32[]{:S(2)}) async-start(), calls=%async_computation.1 | async-start | bytes 5242880 | tf_op jit(solution)/shard_map/all_gather | solution.py:37
  39.6 6.3 %copy-start.2 = (f32[1,512,512]{2,1,0:T(8,128)S(1)}, f32[1,512,512]{2,1,0:T(8,128)}, u32[]{:S(2)}) copy-start(f32[1,512,512]{2,1,0:T(8,128)} %all-gather.11.cloned.1.call-done) | copy-start | bytes 3145732
  41.8 4.2 collective-permute-start.1
  43.9 5.0 %collective-permute-start = (bf16[512,512]{1,0:T(8,128)(2,1)}, bf16[512,512]{1,0:T(8,128)(2,1)}, u32[]{:S(2)}, u32[]{:S(2)}) collective-permute-start(bf16[512,512]{1,0:T(8,128)(2,1)} %bitcast_convert_fusion), channel_id=1, source_target_pairs={{4,0},{8,4},{12,8},{16,12},{20,16},{24,20},{28,24},{5,1},{9,5},{13... | collective-permute-start | bytes 1572872 | tf_op jit(solution)/shard_map/ppermute | solution.py:12
  60.5 117.1 %all-gather.15.cloned.1.call-start = ((), (), s32[]{:S(2)}) async-start(), calls=%async_computation.2 | async-start | bytes 1310720 | tf_op jit(solution)/shard_map/all_gather | solution.py:30
  61.3 239.1 %all-gather.17.cloned.1.call-start = ((), (), s32[]{:S(2)}) async-start(), calls=%async_computation.3 | async-start | bytes 5242880 | tf_op jit(solution)/shard_map/all_gather | solution.py:37
  195.0 2.8 collective-permute-start.3
  196.4 3.8 collective-permute-start.2
  210.5 232.8 %all-gather.19.cloned.1.call-start = ((), (), s32[]{:S(2)}) async-start(), calls=%async_computation.4 | async-start | bytes 5242880 | tf_op jit(solution)/shard_map/all_gather | solution.py:37
  325.2 17.6 %copy-start.1 = (f32[512,512]{1,0:T(8,128)S(1)}, f32[512,512]{1,0:T(8,128)}, u32[]{:S(2)}) copy-start(f32[512,512]{1,0:T(8,128)} %get-tuple-element.20) | copy-start | bytes 3145732
  339.6 3.3 collective-permute-start.5
  341.5 3.8 collective-permute-start.4
Sparse Core Ops, SparseCore 0:
  8.9 30.6 all-gather.10
  60.6 88.8 all-gather.12
  151.1 26.4 all-gather.14
  210.7 89.6 all-gather.16
  355.7 87.5 all-gather.18
